TPU v7x, 256 devices: a whole 4x4x8 slice. The times are simulated.
256 devices in a mesh: slab: 16 (over x, y), pencil: 16 (over z, core).
Axes of the slice: x: 4, y: 4, z: 8, core: 2. Of those that a mesh axis runs over, the one named last changes fastest.
Arguments:
- charges: bfloat16 [64, 131072], P(None, ('slab', 'pencil')), may hold values from -6 to 6
- cotangent: bfloat16 [64, 131072], P(None, ('slab', 'pencil')), may hold values from -6 to 6
- base_cell: int32 [3, 131072], P(None, ('slab', 'pencil')), may hold values from 0 to 63, as said below
- frac: float32 [3, 131072], P(None, ('slab', 'pencil')), may hold values from 0 to 1
- counts: int32 [256], P(('slab', 'pencil')), may hold values from 256 to 512, as said below
- filter_weights: float32 [32, 64], replicated, may hold values from -6 to 6
Outputs:
- potential: bfloat16 [64, 131072], P(None, ('slab', 'pencil'))
- charge_grad: bfloat16 [64, 131072], P(None, ('slab', 'pencil'))
- filter_grad: float32 [32, 64], replicated
Inputs may be any that keep to these rules, and one draw needn't show every extreme that they name: `base_cell`: slots d * 512 to (d + 1) * 512 - 1 belong to device d = slab index * (pencil axis size) + pencil index; their first cell index lies in the slab index's run of 4 cells and their second in the pencil index's run of 4 cells; the third is any cell. A device's live atoms are its first counts slots; some device's count is 512.
All inputs are finite; a program needn't handle non-finite values.
Results may differ from a plain program's by a relative error of at most 0.013.
Values may be sent and summed in bfloat16 or wider, within the bound.
A program may use at most 128 MiB of HBM per device.

v0:
```python
import jax
import jax.numpy as jnp
from jax import lax
from jax.sharding import PartitionSpec as P

N = 64
C = 64
NB = 32
ENV_SCALE = 40.0
ENV_WIDTH = 16.0


def passed_along(value, axis, steps):
    count = lax.axis_size(axis)
    pairs = [(source, (source + steps) % count) for source in range(count)]
    return lax.ppermute(value, axis, pairs)


def spline_weights(frac):
    remain = 1.0 - frac
    square = frac * frac
    cubed = square * frac
    weight_zero = remain * remain * remain / 6.0
    weight_one = (3.0 * cubed - 6.0 * square + 4.0) / 6.0
    weight_two = (-3.0 * cubed + 3.0 * square + 3.0 * frac + 1.0) / 6.0
    weight_three = cubed / 6.0
    return jnp.stack([weight_zero, weight_one, weight_two, weight_three], axis=1)


def stencil_local(base_cell, frac, live, x_first, y_first, span_y):
    weights = spline_weights(frac)
    offsets = jnp.arange(64, dtype=jnp.int32)
    along_x = jnp.repeat(weights[0], 16, axis=0)
    along_y = jnp.tile(jnp.repeat(weights[1], 4, axis=0), (4, 1))
    along_z = jnp.tile(weights[2], (16, 1))
    stencil = along_x * along_y * along_z * live[None, :]
    local_x = base_cell[0][None, :] - x_first + offsets[:, None] // 16
    local_y = base_cell[1][None, :] - y_first + offsets[:, None] // 4 % 4
    local_z = (base_cell[2][None, :] + offsets[:, None] % 4) % N
    cell_ids = (local_x * (span_y + 3) + local_y) * N + local_z
    return (cell_ids, stencil)


def frequencies(positions):
    return jnp.where(positions < N // 2, positions, positions - N).astype(jnp.float32)


def filter_shells(y_first, z_first, y_count, z_count):
    freq_x = frequencies(jnp.arange(N, dtype=jnp.int32))
    freq_y = frequencies(y_first + jnp.arange(y_count, dtype=jnp.int32))
    freq_z = frequencies(z_first + jnp.arange(z_count, dtype=jnp.int32))
    kappa_sq = (
        freq_x[:, None, None] * freq_x[:, None, None]
        + freq_y[None, :, None] * freq_y[None, :, None]
        + freq_z[None, None, :] * freq_z[None, None, :]
    )
    kappa = jnp.sqrt(kappa_sq)
    envelope = ENV_SCALE * ENV_WIDTH / (ENV_WIDTH + kappa_sq)
    spacing = N / (2.0 * NB)
    centers = (jnp.arange(NB, dtype=jnp.float32) + 0.5) * spacing
    shells = envelope[..., None] * jnp.exp(-jnp.square((kappa[..., None] - centers) / spacing))
    return shells.reshape(N * y_count * z_count, NB)


def dft_tables(length):
    indices = jnp.arange(length, dtype=jnp.int32)
    phases = indices[:, None] * indices[None, :] % length
    angles = phases.astype(jnp.float32) * (2.0 * jnp.pi / length)
    return (jnp.cos(angles), jnp.sin(angles))


def contract(operand, matrix, pattern):
    if operand.dtype == jnp.bfloat16:
        table_high = matrix.astype(jnp.bfloat16)
        table_low = (matrix - table_high.astype(jnp.float32)).astype(jnp.bfloat16)
        first = jnp.einsum(pattern, operand, table_high, preferred_element_type=jnp.float32)
        second = jnp.einsum(pattern, operand, table_low, preferred_element_type=jnp.float32)
        return first + second
    return jnp.einsum(pattern, operand, matrix, precision=lax.Precision.HIGHEST)


def transform(values, pattern, inverse, real_in, real_out):
    cosines, sines = dft_tables(N)
    direction = 1.0 if inverse else -1.0
    factor = 1.0 / N if inverse else 1.0
    if real_in:
        real_part = values
        new_real = contract(real_part, cosines, pattern)
        new_imag = direction * contract(real_part, sines, pattern)
    else:
        halfway = values.shape[-1] // 2
        real_part = values[..., :halfway]
        imag_part = values[..., halfway:]
        new_real = contract(real_part, cosines, pattern) - direction * contract(
            imag_part, sines, pattern
        )
        if real_out:
            return new_real * factor
        new_imag = contract(imag_part, cosines, pattern) + direction * contract(
            real_part, sines, pattern
        )
    return jnp.concatenate([new_real, new_imag], axis=-1) * factor


def spread(values, cell_ids, stencil, span_x, span_y, blocks_run):
    channels = values.shape[1]
    total_cells = (span_x + 3) * (span_y + 3) * N

    def add_block(number, totals):
        block_vals = values.astype(jnp.float32)
        products = stencil[:, :, None] * block_vals[None, :, :]
        return totals.at[cell_ids.reshape(-1)].add(products.reshape(-1, channels))

    totals = lax.fori_loop(
        0, blocks_run, add_block, jnp.zeros((total_cells, channels), jnp.float32)
    )
    totals = totals.reshape(span_x + 3, span_y + 3, N, channels)
    rim_planes = passed_along(totals[span_x:].astype(jnp.bfloat16), "slab", 1).astype(jnp.float32)
    totals = totals[:span_x].at[:3].add(rim_planes)
    rim_rows = passed_along(totals[:, span_y:].astype(jnp.bfloat16), "pencil", 1).astype(
        jnp.float32
    )
    return totals[:, :span_y].at[:, :3].add(rim_rows)


def interpolate(grid_vals, cell_ids, stencil, blocks_run, block_len, slots):
    ghost_planes = passed_along(grid_vals[:3], "slab", -1)
    grid_vals = jnp.concatenate([grid_vals, ghost_planes], axis=0)
    ghost_rows = passed_along(grid_vals[:, :3], "pencil", -1)
    grid_vals = jnp.concatenate([grid_vals, ghost_rows], axis=1)
    channels = grid_vals.shape[3]
    flattened = grid_vals.reshape(-1, channels)

    def take_block(number, result):
        picked = (
            flattened[cell_ids.reshape(-1)].reshape(64, block_len, channels).astype(jnp.float32)
        )
        summed = jnp.sum(stencil[:, :, None] * picked, axis=0).astype(jnp.bfloat16)
        return summed

    return lax.fori_loop(0, blocks_run, take_block, jnp.zeros((slots, channels), jnp.bfloat16))


def forward_spectrum(density):
    section_one = transform(density, "xyzc,zk->xykc", False, True, False).astype(jnp.bfloat16)

    def along_y(block_vals):
        return transform(block_vals, "xyzc,yk->xkzc", False, False, False).astype(jnp.bfloat16)

    middle = along_y(lax.all_to_all(section_one, "pencil", split_axis=2, concat_axis=1, tiled=True))

    def along_x(block_vals):
        return transform(block_vals, "xyzc,xk->kyzc", False, False, False)

    return along_x(lax.all_to_all(middle, "slab", split_axis=1, concat_axis=0, tiled=True))


def back_to_cells(spectrum):
    section_one = transform(spectrum, "xyzc,xk->kyzc", True, False, False).astype(jnp.bfloat16)

    def along_y(block_vals):
        return transform(block_vals, "xyzc,yk->xkzc", True, False, False).astype(jnp.bfloat16)

    middle = along_y(lax.all_to_all(section_one, "slab", split_axis=0, concat_axis=1, tiled=True))

    def along_z(block_vals):
        return transform(block_vals, "xyzc,zk->xykc", True, False, True).astype(jnp.bfloat16)

    return along_z(lax.all_to_all(middle, "pencil", split_axis=1, concat_axis=2, tiled=True))


def per_device(charges, cotangent, base_cell, frac, counts, filter_weights):
    charges = charges.T
    cotangent = cotangent.T
    slab_index = lax.axis_index("slab")
    pencil_index = lax.axis_index("pencil")
    span_x = N // lax.axis_size("slab")
    span_y = N // lax.axis_size("pencil")
    slots = charges.shape[0]
    block_len = min(512, slots)
    live_count = counts[0]
    live = (jnp.arange(slots, dtype=jnp.int32) < live_count).astype(jnp.float32)
    cell_ids, stencil = stencil_local(
        base_cell, frac, live, slab_index * span_x, pencil_index * span_y, span_y
    )
    blocks_run = slots // block_len
    shells = filter_shells(slab_index * span_x, pencil_index * span_y, span_x, span_y)
    profile = jnp.dot(shells, filter_weights, precision=lax.Precision.HIGHEST).reshape(
        N, span_x, span_y, C
    )
    doubled = jnp.tile(profile, (1, 1, 1, 2))
    spectrum_q = forward_spectrum(spread(charges, cell_ids, stencil, span_x, span_y, blocks_run))
    potential = interpolate(
        back_to_cells(spectrum_q * doubled), cell_ids, stencil, blocks_run, block_len, slots
    )
    spectrum_g = forward_spectrum(spread(cotangent, cell_ids, stencil, span_x, span_y, blocks_run))
    correlation = (
        spectrum_g[..., :C] * spectrum_q[..., :C] + spectrum_g[..., C:] * spectrum_q[..., C:]
    )
    charge_grad = interpolate(
        back_to_cells(spectrum_g * doubled), cell_ids, stencil, blocks_run, block_len, slots
    )
    partial_grad = jnp.dot(
        shells.T, correlation.reshape(-1, C), precision=lax.Precision.HIGHEST
    ) / (N * N * N)
    filter_grad = lax.psum(partial_grad, ("slab", "pencil"))
    return (potential.T, charge_grad.T, filter_grad)


def solution(mesh):
    in_specs = (
        P(None, ("slab", "pencil")),
        P(None, ("slab", "pencil")),
        P(None, ("slab", "pencil")),
        P(None, ("slab", "pencil")),
        P(("slab", "pencil")),
        P(),
    )
    out_specs = (P(None, ("slab", "pencil")), P(None, ("slab", "pencil")), P())
    return jax.shard_map(
        per_device, mesh=mesh, in_specs=in_specs, out_specs=out_specs, check_vma=False
    )
```

profile of v0, /device:TPU:1, one launch (start us, length us, event | category | flops | bytes accessed | tf_op | source)
XLA Modules:
  0.0 876.0 jit_solution(3839491875228261354)
XLA Ops:
  6.2 12.0 %bitcast_multiply_fusion.1 = (f32[32768,64]{1,0:T(8,128)}, f32[32768,64]{1,0:T(8,128)}) fusion(f32[512,64]{1,0:T(8,128)S(1)} %copy.19, f32[32768]{0:T(1024)S(1)} %multiply_multiply_fusion, f32[512,64]{1,0:T(8,128)S(1)} %copy.28), kind=kLoop, calls=%fused_computation.9 | loop fusion | flops 4194304 | bytes 17170432 | tf_op jit(solution)/shard_map/while/body/eval_jaxpr/mul | solution.py:111
  18.2 174.7 %scatter_custom_fusion.1 = f32[3136,64]{1,0:T(8,128)S(1)} fusion(s32[32768]{0:T(1024)S(1)} %bitcast.346, f32[32768,64]{1,0:T(8,128)} %get-tuple-element.117, f32[]{:T(128)} %constant.266.clone.1), kind=kCustom, calls=%fused_computation.96 | custom fusion | flops 2097152 | bytes 803328 | tf_op jit(solution)/shard_map/while/body/eval_jaxpr/scatter-add | solution.py:112
  193.6 2.1 collective-permute-start.4
  195.8 174.7 %scatter_custom_fusion = f32[3136,64]{1,0:T(8,128)S(1)} fusion(s32[32768]{0:T(1024)S(1)} %bitcast.347, f32[32768,64]{1,0:T(8,128)} %get-tuple-element.116, f32[]{:T(128)} %constant.266.clone.1), kind=kCustom, calls=%fused_computation.98 | custom fusion | flops 2097152 | bytes 803328 | tf_op jit(solution)/shard_map/while/body/eval_jaxpr/scatter-add | solution.py:112
  371.2 1.8 collective-permute-start
  380.6 2.1 add_dynamic-update-slice_fusion
  383.7 2.8 collective-permute-start.5
  386.5 1.3 add_dynamic-update-slice_fusion.1
  393.4 9.9 %all-to-all-start.4 = ((bf16[4,4,64,128]{3,1,0,2:T(4,128)(2,1)}), bf16[4,4,64,128]{3,1,0,2:T(4,128)(2,1)S(1)}, u32[]{:S(2)}, u32[]{:S(2)}) async-start(bf16[4,4,64,128]{3,1,0,2:T(4,128)(2,1)} %copy.29), calls=%async_computation.4 | async-start | bytes 524288 | tf_op jit(solution)/shard_map/all_to_all | solution.py:150
  406.8 8.1 all-to-all-done.4
  414.9 3.4 all-to-all-start
  421.5 8.0 all-to-all-done
  432.6 1.4 fusion.17
  434.0 1.4 fusion.19
  437.2 6.0 all-to-all-start.5
  443.3 1.4 fusion.3
  444.7 1.4 fusion.5
  447.9 3.2 all-to-all-done.5
  451.1 3.9 all-to-all-start.1
  457.3 5.1 all-to-all-done.1
  464.4 1.4 fusion.23
  469.8 1.5 fusion.64
  474.7 4.4 all-to-all-start.2
  479.1 1.8 convolution_subtract_fusion
  482.7 3.8 all-to-all-done.2
  486.5 3.6 all-to-all-start.6
  495.8 1.6 all-to-all-done.6
  500.2 1.4 convolution_add_fusion.18
  501.6 1.4 convolution_add_fusion.16
  503.0 1.4 fusion.11
  504.4 1.4 fusion.13
  506.9 8.0 all-to-all-start.3
  515.0 1.4 convolution_add_fusion.4
  516.4 1.4 convolution_add_fusion.2
  520.0 6.7 all-to-all-done.3
  526.7 3.4 all-to-all-start.7
  530.2 1.6 fusion.161
  533.4 7.7 all-to-all-done.7
  541.9 1.4 convolution_add_fusion.14
  543.7 2.3 collective-permute-start.2
  547.7 2.7 collective-permute-done.2
  550.4 1.2 collective-permute-start.3
  551.6 2.9 collective-permute-done.6
  556.8 1.3 fusion.48
  558.1 76.5 %psum.7 = f32[32,64]{1,0:T(8,128)} all-reduce(f32[32,64]{1,0:T(8,128)S(1)} %fusion.48), channel_id=1, replica_groups=mesh['slab'=16,'pencil'=16] {'slab','pencil'}, use_global_device_ids=true, to_apply=%region_4.5 | all-reduce | flops 2048 | bytes 16384 | tf_op jit(solution)/shard_map/psum | solution.py:206
  635.7 114.9 %gather_fusion = bf16[32768,64]{1,0:T(8,128)(2,1)} fusion(bf16[3136,64]{1,0:T(8,128)(2,1)S(1)} %bitcast.273, s32[32768]{0:T(1024)S(1)} %broadcast_clamp_fusion), kind=kCustom, calls=%fused_computation | custom fusion | bytes 8519680 | tf_op jit(solution)/shard_map/while/body/eval_jaxpr/gather | solution.py:136
  751.8 114.9 %gather_fusion.1 = bf16[32768,64]{1,0:T(8,128)(2,1)} fusion(bf16[3136,64]{1,0:T(8,128)(2,1)S(1)} %bitcast.272, s32[32768]{0:T(1024)S(1)} %broadcast_clamp_fusion), kind=kCustom, calls=%fused_computation.1 | custom fusion | bytes 8519680 | tf_op jit(solution)/shard_map/while/body/eval_jaxpr/gather | solution.py:136
  866.7 7.5 fusion
  (173 shorter events, 69.3 us)
Async XLA Ops:
  0.6 376.4 %copy-start = (f32[32,64]{1,0:T(8,128)S(1)}, f32[32,64]{1,0:T(8,128)}, u32[]{:S(2)}) copy-start(f32[32,64]{1,0:T(8,128)} %param.19) | copy-start | bytes 24580
  1.4 0.9 copy-start.10
  2.3 15.9 %copy-start.11 = (f32[512]{0:T(512)}, f32[512]{0:T(512)S(1)}, u32[]{:S(2)}) copy-start(f32[512]{0:T(512)S(1)} %fusion.301) | copy-start | bytes 6148
  6.1 189.7 %copy-start.5 = (s32[32768,1]{0,1:T(1,128)}, s32[32768,1]{0,1:T(1,128)S(1)}, u32[]{:S(2)}) copy-start(s32[32768,1]{0,1:T(1,128)S(1)} %compare_select_fusion) | copy-start | bytes 393220
  193.6 186.9 %collective-permute-start.4 = (bf16[3,7,64,64]{3,2,1,0:T(8,128)(2,1)}, bf16[3,7,64,64]{3,2,1,0:T(8,128)(2,1)}, u32[]{:S(2)}, u32[]{:S(2)}) collective-permute-start(bf16[3,7,64,64]{3,2,1,0:T(8,128)(2,1)} %bitcast.66), channel_id=1, source_target_pairs={{0,16},{16,32},{32,48},{48,64},{64,80},{80,96},{96,112},{112,128},... | collective-permute-start | bytes 516104 | tf_op jit(solution)/shard_map/ppermute | solution.py:16
  371.2 15.2 %collective-permute-start = (bf16[3,7,64,64]{3,2,1,0:T(8,128)(2,1)}, bf16[3,7,64,64]{3,2,1,0:T(8,128)(2,1)}, u32[]{:S(2)}, u32[]{:S(2)}) collective-permute-start(bf16[3,7,64,64]{3,2,1,0:T(8,128)(2,1)} %bitcast.21), channel_id=1, source_target_pairs={{0,16},{16,32},{32,48},{48,64},{64,80},{80,96},{96,112},{112,128},... | collective-permute-start | bytes 516104 | tf_op jit(solution)/shard_map/ppermute | solution.py:16
  375.9 29.1 %copy-start.13 = (f32[32]{0:T(128)}, f32[32]{0:T(128)S(1)}, u32[]{:S(2)}) copy-start(f32[32]{0:T(128)S(1)} %iota_add_fusion) | copy-start | bytes 388
  377.0 28.7 %copy-start.6 = (f32[64,4,4]{0,2,1:T(4,128)}, f32[64,4,4]{0,2,1:T(4,128)S(1)}, u32[]{:S(2)}) copy-start(f32[64,4,4]{0,2,1:T(4,128)S(1)} %get-tuple-element.128) | copy-start | bytes 12292
  377.0 28.7 %copy-start.8 = (f32[64,4,4]{0,2,1:T(4,128)}, f32[64,4,4]{0,2,1:T(4,128)S(1)}, u32[]{:S(2)}) copy-start(f32[64,4,4]{0,2,1:T(4,128)S(1)} %get-tuple-element.129) | copy-start | bytes 12292
  383.7 6.1 collective-permute-start.5
  388.9 14.4 %collective-permute-start.1 = (bf16[4,3,64,64]{3,2,1,0:T(8,128)(2,1)S(1)}, bf16[4,3,64,64]{3,2,1,0:T(8,128)(2,1)}, u32[]{:S(2)}, u32[]{:S(2)}) collective-permute-start(bf16[4,3,64,64]{3,2,1,0:T(8,128)(2,1)S(1)} %slice.473), channel_id=1, source_target_pairs={{0,1},{1,2},{2,3},{3,4},{4,5},{5,6},{6,7},{7,8},{8,9},{9,10},{10,1... | collective-permute-start | bytes 294920 | tf_op jit(solution)/shard_map/ppermute | solution.py:16
  393.4 21.5 %all-to-all-start.4 = ((bf16[4,4,64,128]{3,1,0,2:T(4,128)(2,1)}), bf16[4,4,64,128]{3,1,0,2:T(4,128)(2,1)S(1)}, u32[]{:S(2)}, u32[]{:S(2)}) async-start(bf16[4,4,64,128]{3,1,0,2:T(4,128)(2,1)} %copy.29), calls=%async_computation.4 | async-start | bytes 524288 | tf_op jit(solution)/shard_map/all_to_all | solution.py:150
  414.9 14.6 %all-to-all-start = ((bf16[4,4,64,128]{3,1,0,2:T(4,128)(2,1)}), bf16[4,4,64,128]{3,1,0,2:T(4,128)(2,1)S(1)}, u32[]{:S(2)}, u32[]{:S(2)}) async-start(bf16[4,4,64,128]{3,1,0,2:T(4,128)(2,1)} %copy.20), calls=%async_computation | async-start | bytes 524288 | tf_op jit(solution)/shard_map/all_to_all | solution.py:150
  437.2 13.9 %all-to-all-start.5 = ((bf16[4,64,4,128]{3,2,0,1:T(4,128)(2,1)}), bf16[4,64,4,128]{3,2,0,1:T(4,128)(2,1)S(1)}, u32[]{:S(2)}, u32[]{:S(2)}) async-start(bf16[4,64,4,128]{3,2,0,1:T(4,128)(2,1)} %copy.31), calls=%async_computation.5 | async-start | bytes 524288 | tf_op jit(solution)/shard_map/all_to_all | solution.py:155
  451.1 11.3 %all-to-all-start.1 = ((bf16[4,64,4,128]{3,2,0,1:T(4,128)(2,1)}), bf16[4,64,4,128]{3,2,0,1:T(4,128)(2,1)S(1)}, u32[]{:S(2)}, u32[]{:S(2)}) async-start(bf16[4,64,4,128]{3,2,0,1:T(4,128)(2,1)} %copy.22), calls=%async_computation.1 | async-start | bytes 524288 | tf_op jit(solution)/shard_map/all_to_all | solution.py:155
  474.7 11.9 %all-to-all-start.2 = ((bf16[64,4,4,128]{3,2,1,0:T(4,128)(2,1)}), bf16[64,4,4,128]{3,2,1,0:T(4,128)(2,1)}, u32[]{:S(2)}, u32[]{:S(2)}) async-start(bf16[64,4,4,128]{3,2,1,0:T(4,128)(2,1)} %copy.24), calls=%async_computation.2 | async-start | bytes 524288 | tf_op jit(solution)/shard_map/all_to_all | solution.py:164
  486.5 10.9 %all-to-all-start.6 = ((bf16[64,4,4,128]{3,2,1,0:T(4,128)(2,1)}), bf16[64,4,4,128]{3,2,1,0:T(4,128)(2,1)S(1)}, u32[]{:S(2)}, u32[]{:S(2)}) async-start(bf16[64,4,4,128]{3,2,1,0:T(4,128)(2,1)} %copy.33), calls=%async_computation.6 | async-start | bytes 524288 | tf_op jit(solution)/shard_map/all_to_all | solution.py:164
  501.6 28.6 %copy-start.12 = (f32[512]{0:T(512)S(1)}, f32[512]{0:T(512)}, u32[]{:S(2)}) copy-start(f32[512]{0:T(512)} %copy-done.11) | copy-start | bytes 6148
  506.9 19.8 %all-to-all-start.3 = ((bf16[4,64,4,128]{3,2,0,1:T(4,128)(2,1)}), bf16[4,64,4,128]{3,2,0,1:T(4,128)(2,1)S(1)}, u32[]{:S(2)}, u32[]{:S(2)}) async-start(bf16[4,64,4,128]{3,2,0,1:T(4,128)(2,1)} %copy.26), calls=%async_computation.3 | async-start | bytes 524288 | tf_op jit(solution)/shard_map/all_to_all | solution.py:169
  518.5 38.3 %copy-start.7 = (f32[64,4,4]{0,2,1:T(4,128)S(1)}, f32[64,4,4]{0,2,1:T(4,128)}, u32[]{:S(2)}) copy-start(f32[64,4,4]{0,2,1:T(4,128)} %copy-done.6) | copy-start | bytes 12292
  518.5 38.3 %copy-start.9 = (f32[64,4,4]{0,2,1:T(4,128)S(1)}, f32[64,4,4]{0,2,1:T(4,128)}, u32[]{:S(2)}) copy-start(f32[64,4,4]{0,2,1:T(4,128)} %copy-done.8) | copy-start | bytes 12292
  526.7 14.4 %all-to-all-start.7 = ((bf16[4,64,4,128]{3,2,0,1:T(4,128)(2,1)}), bf16[4,64,4,128]{3,2,0,1:T(4,128)(2,1)S(1)}, u32[]{:S(2)}, u32[]{:S(2)}) async-start(bf16[4,64,4,128]{3,2,0,1:T(4,128)(2,1)} %copy.35), calls=%async_computation.7 | async-start | bytes 524288 | tf_op jit(solution)/shard_map/all_to_all | solution.py:169
  543.7 6.6 collective-permute-start.2
  546.8 7.8 collective-permute-start.6
  550.4 84.2 %collective-permute-start.3 = (bf16[7,3,64,64]{3,2,1,0:T(8,128)(2,1)S(1)}, bf16[7,3,64,64]{3,2,1,0:T(8,128)(2,1)}, u32[]{:S(2)}, u32[]{:S(2)}) collective-permute-start(bf16[7,3,64,64]{3,2,1,0:T(8,128)(2,1)S(1)} %pad_maximum_fusion.3), channel_id=1, source_target_pairs={{0,15},{1,0},{2,1},{3,2},{4,3},{5,4},{6,5},{7,6},{8,7},{9,8},{10,9... | collective-permute-start | bytes 516104 | tf_op jit(solution)/shard_map/ppermute | solution.py:16
  554.5 0.7 copy-start.2
  556.0 194.6 %collective-permute-start.7 = (bf16[7,3,64,64]{3,2,1,0:T(8,128)(2,1)}, bf16[7,3,64,64]{3,2,1,0:T(8,128)(2,1)}, u32[]{:S(2)}, u32[]{:S(2)}) collective-permute-start(bf16[7,3,64,64]{3,2,1,0:T(8,128)(2,1)} %pad_maximum_fusion.2), channel_id=1, source_target_pairs={{0,15},{1,0},{2,1},{3,2},{4,3},{5,4},{6,5},{7,6},{8,7},{9,8},{10,9... | collective-permute-start | bytes 516104 | tf_op jit(solution)/shard_map/ppermute | solution.py:16
  635.7 114.9 %copy-start.3 = (bf16[3,4,64,64]{3,2,1,0:T(8,128)(2,1)S(1)}, bf16[3,4,64,64]{3,2,1,0:T(8,128)(2,1)}, u32[]{:S(2)}) copy-start(bf16[3,4,64,64]{3,2,1,0:T(8,128)(2,1)} %copy-done.2) | copy-start | bytes 294916
  751.8 114.9 %copy-start.4 = (f32[64,512]{1,0:T(8,128)S(1)}, f32[64,512]{1,0:T(8,128)}, u32[]{:S(2)}) copy-start(f32[64,512]{1,0:T(8,128)} %fusion.161) | copy-start | bytes 393220
  866.7 9.0 %copy-start.1 = (f32[32,64]{1,0:T(8,128)S(1)}, f32[32,64]{1,0:T(8,128)}, u32[]{:S(2)}) copy-start(f32[32,64]{1,0:T(8,128)} %param.19) | copy-start | bytes 24580
where the time goes:
time: 884 us; the launch traced here: 876 us
  other arithmetic  386 us (44%)
  local copies, waits for them, and re-layouts  251 us (28%)
  blocking collectives  76.5 us (9%)
  starting transfers between devices  55.5 us (6%)
  matrix products  54.9 us (6%)
  waiting for transfers between devices  49.8 us (6%)
    scatter-add x2, other arithmetic, add_block(): return totals.at[cell_ids.reshape(-1)].add(products.reshape(-1, channels))  349 us
    gather x2, local copies, waits for them, and re-layouts, take_block(): flattened[cell_ids.reshape(-1)].reshape(64, block_len, channels)  230 us
    psum x1, blocking collectives, per_device(): filter_grad = lax.psum(partial_grad, ('slab', 'pencil'))  76.5 us
    dot_general x28, matrix products, contract(): jnp.einsum(pattern, operand, table_low, preferred_element_type=jnp.float32)  22.5 us
    dot_general x28, matrix products, contract(): jnp.einsum(pattern, operand, table_high, preferred_element_type=jnp.float32)  19.5 us
  transfers between devices with their start and end apart: 16, of which 10 were waited for; matrix products, arithmetic and copies ran while one was open for 39% of the time, Pallas kernels for 0%

commit v1 on v0

--- a/solution.py
+++ b/solution.py
@@ -203,7 +203,8 @@
     partial_grad = jnp.dot(
         shells.T, correlation.reshape(-1, C), precision=lax.Precision.HIGHEST
     ) / (N * N * N)
-    filter_grad = lax.psum(partial_grad, ("slab", "pencil"))
+    blocks = lax.all_gather(partial_grad, ("slab", "pencil"))
+    filter_grad = jnp.sum(blocks, axis=0)
     return (potential.T, charge_grad.T, filter_grad)
 
 

time: 884 us -> 809 us (0.915)
  blocking collectives: 76.5 us -> 0 us
  matrix products: 54.9 us -> 40.7 us
  between operations: 2.63 us -> 16 us
  waiting for transfers between devices: 49.8 us -> 59.5 us
    psum x1 -> x0, blocking collectives: 76.5 us -> none  [per_device(): filter_grad = lax.psum(partial_grad, ('slab', 'pencil'))]
  transfers between devices with their start and end apart: 16 -> 17, of which waited for: 10 -> 10; matrix products, arithmetic and copies ran while one was open for 39% -> 57% of each run, Pallas kernels for 0% -> 0%
where the time goes in v1:
time: 809 us; the launch traced here: 801 us
  other arithmetic  384 us (47%)
  local copies, waits for them, and re-layouts  248 us (31%)
  waiting for transfers between devices  59.5 us (7%)
  starting transfers between devices  52.7 us (7%)
  matrix products  40.7 us (5%)
  between operations  16 us (2%)
    scatter-add x2, other arithmetic, add_block(): return totals.at[cell_ids.reshape(-1)].add(products.reshape(-1, channels))  349 us
    gather x2, local copies, waits for them, and re-layouts, take_block(): flattened[cell_ids.reshape(-1)].reshape(64, block_len, channels)  228 us
    all_to_all x2, waiting for transfers between devices, back_to_cells(): lax.all_to_all(middle, 'pencil', split_axis=1, concat_axis=2, tiled=True)  17.5 us
    all_to_all x2, waiting for transfers between devices, forward_spectrum(): lax.all_to_all(section_one, 'pencil', split_axis=2, concat_axis=1, tiled=...  17 us
  transfers between devices with their start and end apart: 17, of which 10 were waited for; matrix products, arithmetic and copies ran while one was open for 57% of the time, Pallas kernels for 0%

profile of v1, /device:TPU:1, one launch (start us, length us, event | category | flops | bytes accessed | tf_op | source)
XLA Modules:
  0.0 801.2 jit_solution(4918861347492805706)
XLA Ops:
  12.7 12.0 %bitcast_multiply_fusion.1 = (f32[32768,64]{1,0:T(8,128)}, f32[32768,64]{1,0:T(8,128)}) fusion(f32[512,64]{1,0:T(8,128)S(1)} %copy.19, f32[32768]{0:T(1024)S(1)} %multiply_multiply_fusion, f32[512,64]{1,0:T(8,128)S(1)} %copy.28), kind=kLoop, calls=%fused_computation.9 | loop fusion | flops 4194304 | bytes 17170432 | tf_op jit(solution)/shard_map/while/body/eval_jaxpr/mul | solution.py:111
  24.7 174.7 %scatter_custom_fusion.1 = f32[3136,64]{1,0:T(8,128)S(1)} fusion(s32[32768]{0:T(1024)S(1)} %bitcast.349, f32[32768,64]{1,0:T(8,128)} %get-tuple-element.117, f32[]{:T(128)} %constant.267.clone.1), kind=kCustom, calls=%fused_computation.96 | custom fusion | flops 2097152 | bytes 803328 | tf_op jit(solution)/shard_map/while/body/eval_jaxpr/scatter-add | solution.py:112
  200.1 2.1 collective-permute-start.4
  202.3 174.7 %scatter_custom_fusion = f32[3136,64]{1,0:T(8,128)S(1)} fusion(s32[32768]{0:T(1024)S(1)} %bitcast.350, f32[32768,64]{1,0:T(8,128)} %get-tuple-element.116, f32[]{:T(128)} %constant.267.clone.1), kind=kCustom, calls=%fused_computation.98 | custom fusion | flops 2097152 | bytes 803328 | tf_op jit(solution)/shard_map/while/body/eval_jaxpr/scatter-add | solution.py:112
  377.7 1.7 collective-permute-start
  383.2 1.1 fusion.74
  384.6 1.4 tile.35
  386.8 2.1 add_dynamic-update-slice_fusion
  390.0 2.8 collective-permute-start.5
  392.7 1.3 add_dynamic-update-slice_fusion.1
  394.0 1.1 slice.316
  395.2 1.1 collective-permute-start.1
  396.2 1.0 fusion.72
  399.8 9.8 %all-to-all-start.4 = ((bf16[4,4,64,128]{3,1,0,2:T(4,128)(2,1)}), bf16[4,4,64,128]{3,1,0,2:T(4,128)(2,1)S(1)}, u32[]{:S(2)}, u32[]{:S(2)}) async-start(bf16[4,4,64,128]{3,1,0,2:T(4,128)(2,1)} %copy.29), calls=%async_computation.4 | async-start | bytes 524288 | tf_op jit(solution)/shard_map/all_to_all | solution.py:150
  412.1 9.0 %all-to-all-done.4 = bf16[4,4,64,128]{3,1,0,2:T(4,128)(2,1)S(1)} async-done(((bf16[4,4,64,128]{3,1,0,2:T(4,128)(2,1)}), bf16[4,4,64,128]{3,1,0,2:T(4,128)(2,1)S(1)}, u32[]{:S(2)}, u32[]{:S(2)}) %all-to-all-start.4) | async-done | bytes 262176 | tf_op jit(solution)/shard_map/all_to_all | solution.py:150
  421.2 3.4 all-to-all-start
  424.7 1.2 fusion.115
  426.2 1.2 fusion.118
  427.8 8.0 all-to-all-done
  436.6 1.1 fusion.154
  438.1 1.4 fusion.17
  439.5 1.4 fusion.19
  442.7 6.0 all-to-all-start.5
  449.1 1.4 fusion.5
  452.3 4.3 all-to-all-done.5
  456.6 3.9 all-to-all-start.1
  462.1 5.8 all-to-all-done.1
  472.4 1.9 fusion.48
  474.2 1.4 maximum_multiply_fusion
  481.2 3.8 all-to-all-start.2
  487.6 4.8 all-to-all-done.2
  492.4 3.6 all-to-all-start.6
  496.1 1.2 fusion.127
  497.6 1.1 fusion.130
  499.2 4.2 all-to-all-done.6
  504.5 1.4 convolution_add_fusion.18
  505.9 1.4 convolution_add_fusion.16
  509.2 8.1 %all-to-all-start.3 = ((bf16[4,64,4,128]{3,2,0,1:T(4,128)(2,1)}), bf16[4,64,4,128]{3,2,0,1:T(4,128)(2,1)S(1)}, u32[]{:S(2)}, u32[]{:S(2)}) async-start(bf16[4,64,4,128]{3,2,0,1:T(4,128)(2,1)} %copy.26), calls=%async_computation.3 | async-start | bytes 524288 | tf_op jit(solution)/shard_map/all_to_all | solution.py:169
  520.2 8.8 %all-to-all-done.3 = bf16[4,64,4,128]{3,2,0,1:T(4,128)(2,1)S(1)} async-done(((bf16[4,64,4,128]{3,2,0,1:T(4,128)(2,1)}), bf16[4,64,4,128]{3,2,0,1:T(4,128)(2,1)S(1)}, u32[]{:S(2)}, u32[]{:S(2)}) %all-to-all-start.3) | async-done | bytes 262176 | tf_op jit(solution)/shard_map/all_to_all | solution.py:169
  529.0 3.4 all-to-all-start.7
  534.0 1.1 collective-permute-start.2
  535.2 8.7 %all-to-all-done.7 = bf16[4,64,4,128]{3,2,0,1:T(4,128)(2,1)S(1)} async-done(((bf16[4,64,4,128]{3,2,0,1:T(4,128)(2,1)}), bf16[4,64,4,128]{3,2,0,1:T(4,128)(2,1)S(1)}, u32[]{:S(2)}, u32[]{:S(2)}) %all-to-all-start.7) | async-done | bytes 262176 | tf_op jit(solution)/shard_map/all_to_all | solution.py:169
  545.5 1.1 collective-permute-start.6
  546.8 5.5 collective-permute-done.6
  553.6 114.1 %gather_fusion = bf16[32768,64]{1,0:T(8,128)(2,1)} fusion(bf16[3136,64]{1,0:T(8,128)(2,1)S(1)} %bitcast.274, s32[32768]{0:T(1024)S(1)} %broadcast_clamp_fusion), kind=kCustom, calls=%fused_computation | custom fusion | bytes 8519680 | tf_op jit(solution)/shard_map/while/body/eval_jaxpr/gather | solution.py:136
  667.9 114.1 %gather_fusion.1 = bf16[32768,64]{1,0:T(8,128)(2,1)} fusion(bf16[3136,64]{1,0:T(8,128)(2,1)S(1)} %bitcast.273, s32[32768]{0:T(1024)S(1)} %broadcast_clamp_fusion), kind=kCustom, calls=%fused_computation.1 | custom fusion | bytes 8519680 | tf_op jit(solution)/shard_map/while/body/eval_jaxpr/gather | solution.py:136
  782.0 7.5 fusion
  791.0 3.1 reduce_sum.31
  (168 shorter events, 50.1 us)
Async XLA Ops:
  7.2 376.0 %copy-start = (f32[32,64]{1,0:T(8,128)S(1)}, f32[32,64]{1,0:T(8,128)}, u32[]{:S(2)}) copy-start(f32[32,64]{1,0:T(8,128)} %param.19) | copy-start | bytes 24580
  8.0 0.9 copy-start.6
  8.8 15.9 %copy-start.7 = (f32[512]{0:T(512)}, f32[512]{0:T(512)S(1)}, u32[]{:S(2)}) copy-start(f32[512]{0:T(512)S(1)} %fusion.301) | copy-start | bytes 6148
  200.1 186.7 %collective-permute-start.4 = (bf16[3,7,64,64]{3,2,1,0:T(8,128)(2,1)}, bf16[3,7,64,64]{3,2,1,0:T(8,128)(2,1)}, u32[]{:S(2)}, u32[]{:S(2)}) collective-permute-start(bf16[3,7,64,64]{3,2,1,0:T(8,128)(2,1)} %bitcast.66), channel_id=1, source_target_pairs={{0,16},{16,32},{32,48},{48,64},{64,80},{80,96},{96,112},{112,128},... | collective-permute-start | bytes 516104 | tf_op jit(solution)/shard_map/ppermute | solution.py:16
  377.7 15.0 %collective-permute-start = (bf16[3,7,64,64]{3,2,1,0:T(8,128)(2,1)}, bf16[3,7,64,64]{3,2,1,0:T(8,128)(2,1)}, u32[]{:S(2)}, u32[]{:S(2)}) collective-permute-start(bf16[3,7,64,64]{3,2,1,0:T(8,128)(2,1)} %bitcast.21), channel_id=1, source_target_pairs={{0,16},{16,32},{32,48},{48,64},{64,80},{80,96},{96,112},{112,128},... | collective-permute-start | bytes 516104 | tf_op jit(solution)/shard_map/ppermute | solution.py:16
  382.4 0.6 copy-start.9
  382.5 0.6 copy-start.2
  382.6 0.6 copy-start.4
  390.0 6.3 collective-permute-start.5
  395.2 14.4 %collective-permute-start.1 = (bf16[4,3,64,64]{3,2,1,0:T(8,128)(2,1)S(1)}, bf16[4,3,64,64]{3,2,1,0:T(8,128)(2,1)S(1)}, u32[]{:S(2)}, u32[]{:S(2)}) collective-permute-start(bf16[4,3,64,64]{3,2,1,0:T(8,128)(2,1)S(1)} %slice.473), channel_id=1, source_target_pairs={{0,1},{1,2},{2,3},{3,4},{4,5},{5,6},{6,7},{7,8},{8,9},{9,10},{10,1... | collective-permute-start | bytes 294920 | tf_op jit(solution)/shard_map/ppermute | solution.py:16
  399.8 21.4 %all-to-all-start.4 = ((bf16[4,4,64,128]{3,1,0,2:T(4,128)(2,1)}), bf16[4,4,64,128]{3,1,0,2:T(4,128)(2,1)S(1)}, u32[]{:S(2)}, u32[]{:S(2)}) async-start(bf16[4,4,64,128]{3,1,0,2:T(4,128)(2,1)} %copy.29), calls=%async_computation.4 | async-start | bytes 524288 | tf_op jit(solution)/shard_map/all_to_all | solution.py:150
  421.2 14.6 %all-to-all-start = ((bf16[4,4,64,128]{3,1,0,2:T(4,128)(2,1)}), bf16[4,4,64,128]{3,1,0,2:T(4,128)(2,1)S(1)}, u32[]{:S(2)}, u32[]{:S(2)}) async-start(bf16[4,4,64,128]{3,1,0,2:T(4,128)(2,1)} %copy.20), calls=%async_computation | async-start | bytes 524288 | tf_op jit(solution)/shard_map/all_to_all | solution.py:150
  442.7 13.9 %all-to-all-start.5 = ((bf16[4,64,4,128]{3,2,0,1:T(4,128)(2,1)}), bf16[4,64,4,128]{3,2,0,1:T(4,128)(2,1)S(1)}, u32[]{:S(2)}, u32[]{:S(2)}) async-start(bf16[4,64,4,128]{3,2,0,1:T(4,128)(2,1)} %copy.31), calls=%async_computation.5 | async-start | bytes 524288 | tf_op jit(solution)/shard_map/all_to_all | solution.py:155
  456.6 11.3 %all-to-all-start.1 = ((bf16[4,64,4,128]{3,2,0,1:T(4,128)(2,1)}), bf16[4,64,4,128]{3,2,0,1:T(4,128)(2,1)S(1)}, u32[]{:S(2)}, u32[]{:S(2)}) async-start(bf16[4,64,4,128]{3,2,0,1:T(4,128)(2,1)} %copy.22), calls=%async_computation.1 | async-start | bytes 524288 | tf_op jit(solution)/shard_map/all_to_all | solution.py:155
  460.5 330.5 %all-gather.3.cloned.1.call-start = ((), (), s32[]{:S(2)}) async-start(), calls=%async_computation.8 | async-start | bytes 4210688 | tf_op jit(solution)/shard_map/all_gather | solution.py:206
  461.7 10.7 %copy-start.3 = (f32[64,4,4]{0,2,1:T(4,128)S(1)}, f32[64,4,4]{0,2,1:T(4,128)}, u32[]{:S(2)}) copy-start(f32[64,4,4]{0,2,1:T(4,128)} %copy-done.2) | copy-start | bytes 12292
  461.7 10.7 %copy-start.5 = (f32[64,4,4]{0,2,1:T(4,128)S(1)}, f32[64,4,4]{0,2,1:T(4,128)}, u32[]{:S(2)}) copy-start(f32[64,4,4]{0,2,1:T(4,128)} %copy-done.4) | copy-start | bytes 12292
  481.2 11.2 %all-to-all-start.2 = ((bf16[64,4,4,128]{3,2,1,0:T(4,128)(2,1)}), bf16[64,4,4,128]{3,2,1,0:T(4,128)(2,1)S(1)}, u32[]{:S(2)}, u32[]{:S(2)}) async-start(bf16[64,4,4,128]{3,2,1,0:T(4,128)(2,1)} %copy.24), calls=%async_computation.2 | async-start | bytes 524288 | tf_op jit(solution)/shard_map/all_to_all | solution.py:164
  492.4 11.0 %all-to-all-start.6 = ((bf16[64,4,4,128]{3,2,1,0:T(4,128)(2,1)}), bf16[64,4,4,128]{3,2,1,0:T(4,128)(2,1)S(1)}, u32[]{:S(2)}, u32[]{:S(2)}) async-start(bf16[64,4,4,128]{3,2,1,0:T(4,128)(2,1)} %copy.33), calls=%async_computation.6 | async-start | bytes 524288 | tf_op jit(solution)/shard_map/all_to_all | solution.py:164
  509.2 19.9 %all-to-all-start.3 = ((bf16[4,64,4,128]{3,2,0,1:T(4,128)(2,1)}), bf16[4,64,4,128]{3,2,0,1:T(4,128)(2,1)S(1)}, u32[]{:S(2)}, u32[]{:S(2)}) async-start(bf16[4,64,4,128]{3,2,0,1:T(4,128)(2,1)} %copy.26), calls=%async_computation.3 | async-start | bytes 524288 | tf_op jit(solution)/shard_map/all_to_all | solution.py:169
  518.7 34.2 %copy-start.8 = (f32[512]{0:T(512)S(1)}, f32[512]{0:T(512)}, u32[]{:S(2)}) copy-start(f32[512]{0:T(512)} %copy-done.7) | copy-start | bytes 6148
  529.0 14.9 %all-to-all-start.7 = ((bf16[4,64,4,128]{3,2,0,1:T(4,128)(2,1)}), bf16[4,64,4,128]{3,2,0,1:T(4,128)(2,1)S(1)}, u32[]{:S(2)}, u32[]{:S(2)}) async-start(bf16[4,64,4,128]{3,2,0,1:T(4,128)(2,1)} %copy.35), calls=%async_computation.7 | async-start | bytes 524288 | tf_op jit(solution)/shard_map/all_to_all | solution.py:169
  534.0 12.5 %collective-permute-start.2 = (bf16[3,4,64,64]{3,2,1,0:T(8,128)(2,1)S(1)}, bf16[3,4,64,64]{3,2,1,0:T(8,128)(2,1)S(1)}, u32[]{:S(2)}, u32[]{:S(2)}) collective-permute-start(bf16[3,4,64,64]{3,2,1,0:T(8,128)(2,1)S(1)} %slice.312), channel_id=1, source_target_pairs={{0,240},{16,0},{32,16},{48,32},{64,48},{80,64},{96,80},{112,96},{1... | collective-permute-start | bytes 294920 | tf_op jit(solution)/shard_map/ppermute | solution.py:16
  545.5 6.8 collective-permute-start.6
  546.7 6.8 collective-permute-start.3
  552.3 115.4 %collective-permute-start.7 = (bf16[7,3,64,64]{3,2,1,0:T(8,128)(2,1)S(1)}, bf16[7,3,64,64]{3,2,1,0:T(8,128)(2,1)S(1)}, u32[]{:S(2)}, u32[]{:S(2)}) collective-permute-start(bf16[7,3,64,64]{3,2,1,0:T(8,128)(2,1)S(1)} %pad_maximum_fusion.2), channel_id=1, source_target_pairs={{0,15},{1,0},{2,1},{3,2},{4,3},{5,4},{6,5},{7,6},{8,7},{9,8},{10,9... | collective-permute-start | bytes 516104 | tf_op jit(solution)/shard_map/ppermute | solution.py:16
  782.0 12.1 %copy-start.1 = (f32[32,64]{1,0:T(8,128)S(1)}, f32[32,64]{1,0:T(8,128)}, u32[]{:S(2)}) copy-start(f32[32,64]{1,0:T(8,128)} %param.19) | copy-start | bytes 24580
Sparse Core Ops, SparseCore 0:
  478.7 111.7 all-gather.2
